TPU v7x, 32 devices: a whole 2x2x4 slice. The times are simulated.
32 devices in a mesh: ctx: 8 (over z, x), fsdp: 4 (over y, core).
Axes of the slice: x: 2, y: 2, z: 4, core: 2. Of those that a mesh axis runs over, the one named last changes fastest.
Arguments:
- inputs: bfloat16 [4, 4096, 768], P('fsdp', 'ctx'), may hold values from -6 to 6
- doc_starts: int32 [4, 8], P('fsdp'), may hold values from 0 to 4095, as said below
- qkv_weight: bfloat16 [768, 2304], P('fsdp'), may hold values from -0.21875 to 0.21875
- query_bias: bfloat16 [768], P('fsdp'), may hold values from -3 to 3
- value_bias: bfloat16 [768], P('fsdp'), may hold values from -3 to 3
- out_weight: bfloat16 [768, 768], P('fsdp'), may hold values from -2 to 2
- out_bias: bfloat16 [768], P('fsdp'), may hold values from -2 to 2
- norm1_gain: bfloat16 [768], P('fsdp'), may hold values from 0.25 to 1.75
- norm1_bias: bfloat16 [768], P('fsdp'), may hold values from -2 to 2
- in_weight: bfloat16 [768, 3072], P('fsdp'), may hold values from -0.21875 to 0.21875
- in_bias: bfloat16 [3072], P('fsdp'), may hold values from -3 to 3
- back_weight: bfloat16 [3072, 768], P('fsdp'), may hold values from -0.109375 to 0.109375
- back_bias: bfloat16 [768], P('fsdp'), may hold values from -2 to 2
- norm2_gain: bfloat16 [768], P('fsdp'), may hold values from 0.25 to 1.75
- norm2_bias: bfloat16 [768], P('fsdp'), may hold values from -2 to 2
- cotangent: bfloat16 [4, 4096, 768], P('fsdp', 'ctx'), may hold values from -6 to 6
Outputs:
- output: bfloat16 [4, 4096, 768], P('fsdp', 'ctx')
- input_grad: float32 [4, 4096, 768], P('fsdp', 'ctx')
- qkv_weight_grad: float32 [768, 2304], P('fsdp')
- query_bias_grad: float32 [768], P('fsdp')
- value_bias_grad: float32 [768], P('fsdp')
- out_weight_grad: float32 [768, 768], P('fsdp')
- out_bias_grad: float32 [768], P('fsdp')
- norm1_gain_grad: float32 [768], P('fsdp')
- norm1_bias_grad: float32 [768], P('fsdp')
- in_weight_grad: float32 [768, 3072], P('fsdp')
- in_bias_grad: float32 [3072], P('fsdp')
- back_weight_grad: float32 [3072, 768], P('fsdp')
- back_bias_grad: float32 [768], P('fsdp')
- norm2_gain_grad: float32 [768], P('fsdp')
- norm2_bias_grad: float32 [768], P('fsdp')
Inputs may be any that keep to these rules, and one draw needn't show every extreme that they name: `doc_starts`: row s lists the first positions of the 8 documents of stream s in increasing order, all different; the first is 0 and the last is 4095, a one-token document at the stream's end. A document runs from its start to the next start.
All inputs are finite; a program needn't handle non-finite values.
Results may differ from a plain program's by a relative error of at most 0.022.
Values may be sent and summed in bfloat16 or wider, within the bound.
No kernel may reach another device: no remote copies, remote signals or barrier semaphores. Data moves between devices by JAX's collectives and lax.ppermute only.
A program may use at most 192 MiB of HBM per device.

v0:
```python
from functools import partial
import math
import jax
import jax.numpy as jnp
from jax import lax
from jax.sharding import PartitionSpec as P

H = 12
HD = 64
EPSILON = 1e-05
NEGATIVE = -1e30


def layer_norm(resid, gain, shift):
    centre = jnp.mean(resid, axis=-1, keepdims=True)
    centred = resid - centre
    spread = jnp.mean(centred * centred, axis=-1, keepdims=True)
    return centred * lax.rsqrt(spread + EPSILON) * gain + shift


def doc_index(starts, positions):
    return jnp.sum((starts[None, :] <= positions[:, None]).astype(jnp.int32), axis=1) - 1


def over_blocks(block_step, carry, key_rows, value_rows):
    total_rows = key_rows.shape[0]
    size = math.gcd(total_rows, 512)
    count = total_rows // size
    width = key_rows.shape[1]
    key_blocks = key_rows.reshape(count, size, width)
    value_blocks = value_rows.reshape(count, size, width)
    offsets = size * jnp.arange(count, dtype=jnp.int32)

    def inner(state, element):
        offset, key_block, value_block = element
        return (block_step(state, key_block, value_block, offset), None)

    carry, unused = lax.scan(inner, carry, (offsets, key_blocks, value_blocks))
    return carry


def fold_pieces(block_step, carry, piece):
    return over_blocks(block_step, carry, piece[0], piece[1])


def guarded(block_core, starts):

    def wrapped(state, key_block, value_block, offset):
        key_docs = doc_index(starts, offset + jnp.arange(key_block.shape[0], dtype=jnp.int32))
        return block_core(state, key_block, value_block, key_docs, offset)

    return wrapped


def forward_core(query_heads, query_docs, state, key_block, value_block, key_docs, offset):
    best, total, accum = state
    block_len = key_block.shape[0]
    head_count, head_size = (query_heads.shape[1], query_heads.shape[2])
    key_heads = key_block.reshape(block_len, head_count, head_size)
    value_heads = value_block.reshape(block_len, head_count, head_size)
    allowed = (query_docs[:, None] == key_docs[None, :])[None]
    scores = jnp.einsum("qhd,khd->hqk", query_heads, key_heads, preferred_element_type=jnp.float32)
    scores = jnp.where(allowed, scores * head_size ** (-0.5), NEGATIVE)
    new_best = jnp.maximum(best, jnp.max(scores, axis=-1))
    weights = jnp.where(allowed, jnp.exp(scores - new_best[:, :, None]), 0.0)
    shrink = jnp.exp(best - new_best)
    total = total * shrink + jnp.sum(weights, axis=-1)
    update = jnp.einsum(
        "hqk,khd->qhd",
        weights.astype(jnp.bfloat16),
        value_heads,
        preferred_element_type=jnp.float32,
    )
    accum = accum * jnp.transpose(shrink)[:, :, None] + update
    return (new_best, total, accum)


def backward_core(
    query_heads,
    query_docs,
    grad_heads,
    log_total,
    delta,
    state,
    key_block,
    value_block,
    key_docs,
    offset,
):
    grad_query, key_terms = state
    block_len = key_block.shape[0]
    head_count, head_size = (query_heads.shape[1], query_heads.shape[2])
    key_heads = key_block.reshape(block_len, head_count, head_size)
    value_heads = value_block.reshape(block_len, head_count, head_size)
    allowed = (query_docs[:, None] == key_docs[None, :])[None]
    scores = jnp.einsum("qhd,khd->hqk", query_heads, key_heads, preferred_element_type=jnp.float32)
    scores = jnp.where(allowed, scores * head_size ** (-0.5), NEGATIVE)
    probs = jnp.where(allowed, jnp.exp(scores - log_total[:, :, None]), 0.0)
    d_probs = jnp.einsum(
        "qhd,khd->hqk", grad_heads, value_heads, preferred_element_type=jnp.float32
    )
    d_scores = (probs * (d_probs - delta[:, :, None]) * head_size ** (-0.5)).astype(jnp.bfloat16)
    grad_query = grad_query + jnp.einsum(
        "hqk,khd->qhd", d_scores, key_heads, preferred_element_type=jnp.float32
    )
    key_grad = jnp.einsum("hqk,qhd->khd", d_scores, query_heads, preferred_element_type=jnp.float32)
    value_grad = jnp.einsum(
        "hqk,qhd->khd", probs.astype(jnp.bfloat16), grad_heads, preferred_element_type=jnp.float32
    )
    joined = jnp.concatenate(
        [
            key_grad.reshape(block_len, head_count * head_size),
            value_grad.reshape(block_len, head_count * head_size),
        ],
        axis=1,
    )
    key_terms = lax.dynamic_update_slice(key_terms, joined, (offset, 0))
    return (grad_query, key_terms)


def body(
    inputs,
    doc_starts,
    qkv_weight,
    query_bias,
    value_bias,
    out_weight,
    out_bias,
    norm1_gain,
    norm1_bias,
    in_weight,
    in_bias,
    back_weight,
    back_bias,
    norm2_gain,
    norm2_bias,
    cotangent,
):
    (
        qkv_full,
        query_shift,
        value_shift,
        out_full,
        out_shift,
        gain_one,
        shift_one,
        in_full,
        in_shift,
        back_full,
        back_shift,
        gain_two,
        shift_two,
    ) = (
        lax.all_gather(qkv_weight, "fsdp", axis=0, tiled=True),
        lax.all_gather(query_bias, "fsdp", axis=0, tiled=True),
        lax.all_gather(value_bias, "fsdp", axis=0, tiled=True),
        lax.all_gather(out_weight, "fsdp", axis=0, tiled=True),
        lax.all_gather(out_bias, "fsdp", axis=0, tiled=True),
        lax.all_gather(norm1_gain, "fsdp", axis=0, tiled=True),
        lax.all_gather(norm1_bias, "fsdp", axis=0, tiled=True),
        lax.all_gather(in_weight, "fsdp", axis=0, tiled=True),
        lax.all_gather(in_bias, "fsdp", axis=0, tiled=True),
        lax.all_gather(back_weight, "fsdp", axis=0, tiled=True),
        lax.all_gather(back_bias, "fsdp", axis=0, tiled=True),
        lax.all_gather(norm2_gain, "fsdp", axis=0, tiled=True),
        lax.all_gather(norm2_bias, "fsdp", axis=0, tiled=True),
    )
    tokens = inputs[0]
    local_rows = tokens.shape[0]
    model = tokens.shape[1]
    stream_len = local_rows * lax.axis_size("ctx")
    starts = doc_starts[0]
    query_docs = doc_index(
        starts, lax.axis_index("ctx") * local_rows + jnp.arange(local_rows, dtype=jnp.int32)
    )
    projected = jnp.dot(tokens, qkv_full, preferred_element_type=jnp.float32)
    query_low = (projected[:, :model] + query_shift.astype(jnp.float32)).astype(jnp.bfloat16)
    key_low = projected[:, model : 2 * model].astype(jnp.bfloat16)
    value_low = (projected[:, 2 * model :] + value_shift.astype(jnp.float32)).astype(jnp.bfloat16)
    query_heads = query_low.reshape(local_rows, H, HD)
    forward_block = guarded(partial(forward_core, query_heads, query_docs), starts)
    initial = (
        jnp.full((H, local_rows), NEGATIVE, jnp.float32),
        jnp.zeros((H, local_rows), jnp.float32),
        jnp.zeros((local_rows, H, HD), jnp.float32),
    )
    best, total, accum = fold_pieces(
        forward_block,
        initial,
        (
            lax.all_gather(key_low, "ctx", axis=0, tiled=True),
            lax.all_gather(value_low, "ctx", axis=0, tiled=True),
        ),
    )
    log_total = best + jnp.log(total)
    attended = accum / jnp.transpose(total)[:, :, None]
    attended_low = attended.reshape(local_rows, model).astype(jnp.bfloat16)
    branch = jnp.dot(attended_low, out_full, preferred_element_type=jnp.float32) + out_shift.astype(
        jnp.float32
    )
    hidden, norm1_back = jax.vjp(
        layer_norm,
        tokens.astype(jnp.float32) + branch,
        gain_one.astype(jnp.float32),
        shift_one.astype(jnp.float32),
    )
    hidden_low = hidden.astype(jnp.bfloat16)
    pre_act = jnp.dot(hidden_low, in_full, preferred_element_type=jnp.float32) + in_shift.astype(
        jnp.float32
    )
    activated, gelu_back = jax.vjp(partial(jax.nn.gelu, approximate=False), pre_act)
    act_low = activated.astype(jnp.bfloat16)
    ffn_out = jnp.dot(act_low, back_full, preferred_element_type=jnp.float32) + back_shift.astype(
        jnp.float32
    )
    result, norm2_back = jax.vjp(
        layer_norm, hidden + ffn_out, gain_two.astype(jnp.float32), shift_two.astype(jnp.float32)
    )
    d_resid2, grad_gain_two, grad_shift_two = norm2_back(cotangent[0].astype(jnp.float32))
    d_ffn_low = d_resid2.astype(jnp.bfloat16)
    grad_back_full = jnp.einsum("tf,td->fd", act_low, d_ffn_low, preferred_element_type=jnp.float32)
    grad_back_shift = jnp.sum(d_ffn_low, axis=0, dtype=jnp.float32)
    d_act = jnp.einsum("td,fd->tf", d_ffn_low, back_full, preferred_element_type=jnp.float32)
    d_pre_low = gelu_back(d_act)[0].astype(jnp.bfloat16)
    grad_in_full = jnp.einsum(
        "td,tf->df", hidden_low, d_pre_low, preferred_element_type=jnp.float32
    )
    grad_in_shift = jnp.sum(d_pre_low, axis=0, dtype=jnp.float32)
    d_hidden = d_resid2 + jnp.einsum(
        "tf,df->td", d_pre_low, in_full, preferred_element_type=jnp.float32
    )
    d_resid1, grad_gain_one, grad_shift_one = norm1_back(d_hidden)
    d_branch_low = d_resid1.astype(jnp.bfloat16)
    grad_out_full = jnp.einsum(
        "tc,td->cd", attended_low, d_branch_low, preferred_element_type=jnp.float32
    )
    grad_out_shift = jnp.sum(d_branch_low, axis=0, dtype=jnp.float32)
    d_attended_low = jnp.einsum(
        "td,cd->tc", d_branch_low, out_full, preferred_element_type=jnp.float32
    ).astype(jnp.bfloat16)
    grad_heads = d_attended_low.reshape(local_rows, H, HD)
    delta = jnp.transpose(jnp.sum(grad_heads.astype(jnp.float32) * attended, axis=-1))
    backward_block = guarded(
        partial(backward_core, query_heads, query_docs, grad_heads, log_total, delta), starts
    )
    initial_back = (
        jnp.zeros((local_rows, H, HD), jnp.float32),
        jnp.zeros((stream_len, 2 * model), jnp.float32),
    )
    grad_query, key_terms = fold_pieces(
        backward_block,
        initial_back,
        (
            lax.all_gather(key_low, "ctx", axis=0, tiled=True),
            lax.all_gather(value_low, "ctx", axis=0, tiled=True),
        ),
    )
    key_sums = lax.psum_scatter(
        key_terms.astype(jnp.bfloat16), "ctx", scatter_dimension=0, tiled=True
    ).astype(jnp.float32)
    d_query_low = grad_query.reshape(local_rows, model).astype(jnp.bfloat16)
    d_qkv_low = jnp.concatenate(
        [
            d_query_low,
            key_sums[:, :model].astype(jnp.bfloat16),
            key_sums[:, model:].astype(jnp.bfloat16),
        ],
        axis=1,
    )
    grad_qkv_full = jnp.einsum("td,te->de", tokens, d_qkv_low, preferred_element_type=jnp.float32)
    grad_query_shift = jnp.sum(d_query_low, axis=0, dtype=jnp.float32)
    grad_value_shift = jnp.sum(d_qkv_low[:, 2 * model :], axis=0, dtype=jnp.float32)
    input_grad = d_resid1 + jnp.einsum(
        "te,de->td", d_qkv_low, qkv_full, preferred_element_type=jnp.float32
    )
    shards = (
        lax.psum_scatter(
            grad_qkv_full.astype(jnp.bfloat16), "fsdp", scatter_dimension=0, tiled=True
        ).astype(jnp.float32),
        lax.psum_scatter(
            grad_query_shift.astype(jnp.bfloat16), "fsdp", scatter_dimension=0, tiled=True
        ).astype(jnp.float32),
        lax.psum_scatter(
            grad_value_shift.astype(jnp.bfloat16), "fsdp", scatter_dimension=0, tiled=True
        ).astype(jnp.float32),
        lax.psum_scatter(
            grad_out_full.astype(jnp.bfloat16), "fsdp", scatter_dimension=0, tiled=True
        ).astype(jnp.float32),
        lax.psum_scatter(
            grad_out_shift.astype(jnp.bfloat16), "fsdp", scatter_dimension=0, tiled=True
        ).astype(jnp.float32),
        lax.psum_scatter(
            grad_gain_one.astype(jnp.bfloat16), "fsdp", scatter_dimension=0, tiled=True
        ).astype(jnp.float32),
        lax.psum_scatter(
            grad_shift_one.astype(jnp.bfloat16), "fsdp", scatter_dimension=0, tiled=True
        ).astype(jnp.float32),
        lax.psum_scatter(
            grad_in_full.astype(jnp.bfloat16), "fsdp", scatter_dimension=0, tiled=True
        ).astype(jnp.float32),
        lax.psum_scatter(
            grad_in_shift.astype(jnp.bfloat16), "fsdp", scatter_dimension=0, tiled=True
        ).astype(jnp.float32),
        lax.psum_scatter(
            grad_back_full.astype(jnp.bfloat16), "fsdp", scatter_dimension=0, tiled=True
        ).astype(jnp.float32),
        lax.psum_scatter(
            grad_back_shift.astype(jnp.bfloat16), "fsdp", scatter_dimension=0, tiled=True
        ).astype(jnp.float32),
        lax.psum_scatter(
            grad_gain_two.astype(jnp.bfloat16), "fsdp", scatter_dimension=0, tiled=True
        ).astype(jnp.float32),
        lax.psum_scatter(
            grad_shift_two.astype(jnp.bfloat16), "fsdp", scatter_dimension=0, tiled=True
        ).astype(jnp.float32),
    )
    totals = (
        lax.psum(shards[0].astype(jnp.bfloat16), "ctx").astype(jnp.float32),
        lax.psum(shards[1].astype(jnp.bfloat16), "ctx").astype(jnp.float32),
        lax.psum(shards[2].astype(jnp.bfloat16), "ctx").astype(jnp.float32),
        lax.psum(shards[3].astype(jnp.bfloat16), "ctx").astype(jnp.float32),
        lax.psum(shards[4].astype(jnp.bfloat16), "ctx").astype(jnp.float32),
        lax.psum(shards[5].astype(jnp.bfloat16), "ctx").astype(jnp.float32),
        lax.psum(shards[6].astype(jnp.bfloat16), "ctx").astype(jnp.float32),
        lax.psum(shards[7].astype(jnp.bfloat16), "ctx").astype(jnp.float32),
        lax.psum(shards[8].astype(jnp.bfloat16), "ctx").astype(jnp.float32),
        lax.psum(shards[9].astype(jnp.bfloat16), "ctx").astype(jnp.float32),
        lax.psum(shards[10].astype(jnp.bfloat16), "ctx").astype(jnp.float32),
        lax.psum(shards[11].astype(jnp.bfloat16), "ctx").astype(jnp.float32),
        lax.psum(shards[12].astype(jnp.bfloat16), "ctx").astype(jnp.float32),
    )
    return (
        result.astype(jnp.bfloat16)[None],
        input_grad[None],
        totals[0],
        totals[1],
        totals[2],
        totals[3],
        totals[4],
        totals[5],
        totals[6],
        totals[7],
        totals[8],
        totals[9],
        totals[10],
        totals[11],
        totals[12],
    )


def solution(mesh):
    placed = (
        P("fsdp", "ctx", None),
        P("fsdp", None),
        P("fsdp", None),
        P("fsdp"),
        P("fsdp"),
        P("fsdp", None),
        P("fsdp"),
        P("fsdp"),
        P("fsdp"),
        P("fsdp", None),
        P("fsdp"),
        P("fsdp", None),
        P("fsdp"),
        P("fsdp"),
        P("fsdp"),
        P("fsdp", "ctx", None),
    )
    return jax.shard_map(
        body,
        mesh=mesh,
        in_specs=placed,
        out_specs=(
            P("fsdp", "ctx", None),
            P("fsdp", "ctx", None),
            P("fsdp", None),
            P("fsdp"),
            P("fsdp"),
            P("fsdp", None),
            P("fsdp"),
            P("fsdp"),
            P("fsdp"),
            P("fsdp", None),
            P("fsdp"),
            P("fsdp", None),
            P("fsdp"),
            P("fsdp"),
            P("fsdp"),
        ),
        check_vma=False,
    )
```

profile of v0, /device:TPU:0, one launch (start us, length us, event | category | flops | bytes accessed | tf_op | source)
XLA Modules:
  0.0 1406.1 jit_solution(16714513055918829234)
XLA Ops:
  15.8 13.9 all-reduce.20
  29.7 13.5 all-gather.8.cloned.1.call-done
  61.0 88.8 %all-gather.12.cloned.1.call-done = bf16[4096,768]{1,0:T(8,128)(2,1)} async-done(((bf16[512,768]{1,0:T(8,128)(2,1)}), bf16[4096,768]{1,0:T(8,128)(2,1)}) %all-gather.12.cloned.1.call-update) | async-done | bytes 6291472 | tf_op jit(solution)/shard_map/all_gather | solution.py:192
  149.7 8.6 copy.76
  158.3 91.1 %all-gather.10.cloned.1.call-done = bf16[4096,768]{1,0:T(8,128)(2,1)} async-done(((bf16[512,768]{1,0:T(8,128)(2,1)}), bf16[4096,768]{1,0:T(8,128)(2,1)}) %all-gather.10.cloned.1.call-update) | async-done | bytes 6291472 | tf_op jit(solution)/shard_map/all_gather | solution.py:191
  249.4 8.7 copy.75
  258.1 170.9 %while.32 = (s32[]{:T(128)}, f32[12,512]{1,0:T(8,128)S(1)}, f32[12,512]{1,0:T(8,128)S(1)}, f32[512,12,64]{0,2,1:T(8,128)S(1)}, s32[512]{0:T(512)S(1)}, /*index=5...) while((s32[]{:T(128)}, f32[12,512]{1,0:T(8,128)S(1)}, ...), condition=%wide.region_5.6_spmd.clone, body=%wide.region_1.5_spmd.clone.sunk | while | flops 847692288 | bytes 98187464 | solution.py:38
  261.2 6.6 fusion.120
  267.8 6.5 bitcast_add_fusion.4
  283.0 6.6 fusion.120
  289.6 6.5 bitcast_add_fusion.4
  304.2 6.6 fusion.120
  310.8 7.6 bitcast_add_fusion.4
  326.8 6.6 fusion.120
  333.4 6.6 bitcast_add_fusion.4
  348.0 6.6 fusion.120
  354.6 6.5 bitcast_add_fusion.4
  369.0 6.6 fusion.120
  375.6 6.5 bitcast_add_fusion.4
  390.0 6.6 fusion.120
  396.6 6.5 bitcast_add_fusion.4
  411.0 6.6 fusion.120
  417.6 6.5 bitcast_add_fusion.4
  433.5 21.0 %multiply_convert_fusion = (bf16[512,3072]{1,0:T(8,128)(2,1)}, f32[512,3072]{1,0:T(8,128)}, f32[512,3072]{1,0:T(8,128)}) fusion(f32[3072]{0:T(1024)S(1)} %bitcast.195, bf16[768,3072]{1,0:T(8,128)(2,1)} %all-gather.16.cloned.1.call-done, f32[512,768]{1,0:T(8,128)} %copy-done.12, f32[768]{0:T(1024)S(1)} %convert_element_type.229, ...), kind=kOutput, calls=%fused_computation.47 | convolution fusion | flops 2521694208 | bytes 22042624 | tf_op jit(solution)/shard_map/dot_general | solution.py:208
  454.5 6.5 fusion.61
  465.1 8.7 fusion.53
  484.5 6.1 broadcast_in_dim.113
  490.6 366.8 %while.33 = (s32[]{:T(128)}, f32[512,12,64]{0,2,1:T(8,128)}, bf16[4096,1536]{0,1:T(8,128)(2,1)}, bf16[8,512,768]{1,2,0:T(8,128)(2,1)}, s32[512]{0:T(512)S(1)}, /...) while((s32[]{:T(128)}, f32[512,12,64]{0,2,1:T(8,128)}, ...), condition=%wide.region_17.18_spmd.clone, body=%wide.region_15.17_spmd.clone.sunk | while | flops 2058367488 | bytes 114907512 | solution.py:38
  497.6 5.9 fusion.135
  516.8 14.6 %dynamic_update_slice.8 = bf16[4096,1536]{0,1:T(8,128)(2,1)} dynamic-update-slice(bf16[4096,1536]{0,1:T(8,128)(2,1)} %get-tuple-element.831, bf16[512,1536]{0,1:T(8,128)(2,1)S(1)} %pad_maximum_fusion.7, s32[]{:T(128)S(6)} %select_n.93, s32[]{:T(128)} %constant.145.clone.1..sunk.1) | dynamic-update-slice | bytes 3145732 | tf_op jit(solution)/shard_map/while/body/eval_jaxpr/dynamic_update_slice | solution.py:117
  562.4 14.7 %dynamic_update_slice.8 = bf16[4096,1536]{0,1:T(8,128)(2,1)} dynamic-update-slice(bf16[4096,1536]{0,1:T(8,128)(2,1)} %get-tuple-element.831, bf16[512,1536]{0,1:T(8,128)(2,1)S(1)} %pad_maximum_fusion.7, s32[]{:T(128)S(6)} %select_n.93, s32[]{:T(128)} %constant.145.clone.1..sunk.1) | dynamic-update-slice | bytes 3145732 | tf_op jit(solution)/shard_map/while/body/eval_jaxpr/dynamic_update_slice | solution.py:117
  608.3 14.7 %dynamic_update_slice.8 = bf16[4096,1536]{0,1:T(8,128)(2,1)} dynamic-update-slice(bf16[4096,1536]{0,1:T(8,128)(2,1)} %get-tuple-element.831, bf16[512,1536]{0,1:T(8,128)(2,1)S(1)} %pad_maximum_fusion.7, s32[]{:T(128)S(6)} %select_n.93, s32[]{:T(128)} %constant.145.clone.1..sunk.1) | dynamic-update-slice | bytes 3145732 | tf_op jit(solution)/shard_map/while/body/eval_jaxpr/dynamic_update_slice | solution.py:117
  654.4 14.7 %dynamic_update_slice.8 = bf16[4096,1536]{0,1:T(8,128)(2,1)} dynamic-update-slice(bf16[4096,1536]{0,1:T(8,128)(2,1)} %get-tuple-element.831, bf16[512,1536]{0,1:T(8,128)(2,1)S(1)} %pad_maximum_fusion.7, s32[]{:T(128)S(6)} %select_n.93, s32[]{:T(128)} %constant.145.clone.1..sunk.1) | dynamic-update-slice | bytes 3145732 | tf_op jit(solution)/shard_map/while/body/eval_jaxpr/dynamic_update_slice | solution.py:117
  700.4 14.7 %dynamic_update_slice.8 = bf16[4096,1536]{0,1:T(8,128)(2,1)} dynamic-update-slice(bf16[4096,1536]{0,1:T(8,128)(2,1)} %get-tuple-element.831, bf16[512,1536]{0,1:T(8,128)(2,1)S(1)} %pad_maximum_fusion.7, s32[]{:T(128)S(6)} %select_n.93, s32[]{:T(128)} %constant.145.clone.1..sunk.1) | dynamic-update-slice | bytes 3145732 | tf_op jit(solution)/shard_map/while/body/eval_jaxpr/dynamic_update_slice | solution.py:117
  746.5 14.6 %dynamic_update_slice.8 = bf16[4096,1536]{0,1:T(8,128)(2,1)} dynamic-update-slice(bf16[4096,1536]{0,1:T(8,128)(2,1)} %get-tuple-element.831, bf16[512,1536]{0,1:T(8,128)(2,1)S(1)} %pad_maximum_fusion.7, s32[]{:T(128)S(6)} %select_n.93, s32[]{:T(128)} %constant.145.clone.1..sunk.1) | dynamic-update-slice | bytes 3145732 | tf_op jit(solution)/shard_map/while/body/eval_jaxpr/dynamic_update_slice | solution.py:117
  792.4 14.6 %dynamic_update_slice.8 = bf16[4096,1536]{0,1:T(8,128)(2,1)} dynamic-update-slice(bf16[4096,1536]{0,1:T(8,128)(2,1)} %get-tuple-element.831, bf16[512,1536]{0,1:T(8,128)(2,1)S(1)} %pad_maximum_fusion.7, s32[]{:T(128)S(6)} %select_n.93, s32[]{:T(128)} %constant.145.clone.1..sunk.1) | dynamic-update-slice | bytes 3145732 | tf_op jit(solution)/shard_map/while/body/eval_jaxpr/dynamic_update_slice | solution.py:117
  838.4 13.5 dynamic_update_slice.8
  859.8 203.3 %reduce-scatter.8.cloned.1.call-done = bf16[512,1536]{0,1:T(8,128)(2,1)} async-done(((bf16[4096,1536]{0,1:T(8,128)(2,1)}), bf16[512,1536]{0,1:T(8,128)(2,1)}) %reduce-scatter.8.cloned.1.call-update) | async-done | bytes 1572880 | tf_op jit(solution)/shard_map/reduce_scatter | solution.py:258
  1074.5 7.3 convolution_convert_fusion
  1083.2 6.5 convolution_convert_fusion.1
  1089.9 20.8 %reduce-scatter.16.cloned.1.call-done = bf16[192,2304]{1,0:T(8,128)(2,1)} async-done(((bf16[768,2304]{1,0:T(8,128)(2,1)}), bf16[192,2304]{1,0:T(8,128)(2,1)}) %reduce-scatter.16.cloned.1.call-update) | async-done | bytes 884752
  1113.0 25.9 %reduce-scatter.10.cloned.1.call-done = bf16[192,768]{1,0:T(8,128)(2,1)} async-done(((bf16[768,768]{1,0:T(8,128)(2,1)}), bf16[192,768]{1,0:T(8,128)(2,1)}) %reduce-scatter.10.cloned.1.call-update) | async-done | bytes 294928 | tf_op jit(solution)/shard_map/reduce_scatter | solution.py:286
  1138.9 50.4 %reduce-scatter.14.cloned.1.call-done = bf16[768,768]{1,0:T(8,128)(2,1)} async-done(((bf16[3072,768]{1,0:T(8,128)(2,1)}), bf16[768,768]{1,0:T(8,128)(2,1)}) %reduce-scatter.14.cloned.1.call-update) | async-done | bytes 1179664 | tf_op jit(solution)/shard_map/reduce_scatter | solution.py:304
  1189.3 50.5 %reduce-scatter.12.cloned.1.call-done = bf16[192,3072]{1,0:T(8,128)(2,1)} async-done(((bf16[768,3072]{1,0:T(8,128)(2,1)}), bf16[192,3072]{1,0:T(8,128)(2,1)}) %reduce-scatter.12.cloned.1.call-update) | async-done | bytes 1179664 | tf_op jit(solution)/shard_map/reduce_scatter | solution.py:298
  1243.1 10.3 all-reduce.19
  1254.0 23.2 %all-reduce.17 = (bf16[192]{0:T(256)(128)(2,1)S(1)}, bf16[192]{0:T(256)(128)(2,1)S(1)}, bf16[192]{0:T(256)(128)(2,1)S(1)}, bf16[192]{0:T(256)(128)(2,1)S(1)}, bf...) all-reduce(bf16[192]{0:T(256)(128)(2,1)S(1)} %dynamic-slice.9, ...), channel_id=1, replica_groups=mesh['ctx'=8,'fsdp'=4] {'ctx'}, use_global_device_ids=true, to_apply=%region_23.24 | all-reduce | flops 2304 | bytes 9216 | tf_op jit(solution)/shard_map/psum | solution.py:319
  1283.6 6.2 add_bitcast_fusion
  1289.8 102.2 %all-reduce.23.cloned.1.call-done = (bf16[192,2304]{0,1:T(8,128)(2,1)}, bf16[192,768]{1,0:T(8,128)(2,1)}, bf16[192,3072]{1,0:T(8,128)(2,1)}, bf16[768,768]{1,0:T(8,128)(2,1)}) async-done(((bf16[192,2304]{0,1:T(8,128)(2,1)}, bf16[192,768]{1,0:T(8,128)(2,1)}, bf16[192,3072]{1,0:T(8,128)(2,1)}, bf16[768,768]{1,0:T(8,128)(2,1)}), (bf16[192,2304]{0,1:T(8,128)(2,1)}, bf16[192,768]{1,0:T(8,128)(2,1)}, ...) | async-done | bytes 3538960 | tf_op jit(solution)/shard_map/psum | solution.py:318
  (492 shorter events, 370.4 us)
Async XLA Ops:
  7.2 36.0 %all-gather.8.cloned.1.call-start = ((), (), s32[]{:S(2)}) async-start(), calls=%async_computation.5 | async-start | bytes 4423680 | tf_op jit(solution)/shard_map/all_gather | solution.py:154
  7.9 141.8 %all-gather.12.cloned.1.call-start = ((), (), s32[]{:S(2)}) async-start(), calls=%async_computation.7 | async-start | bytes 7077888 | tf_op jit(solution)/shard_map/all_gather | solution.py:192
  50.8 198.6 %all-gather.10.cloned.1.call-start = ((), (), s32[]{:S(2)}) async-start(), calls=%async_computation.6 | async-start | bytes 7077888 | tf_op jit(solution)/shard_map/all_gather | solution.py:191
  53.3 376.0 %all-gather.14.cloned.1.call-start = ((), (), s32[]{:S(2)}) async-start(), calls=%async_computation.8 | async-start | bytes 1474560 | tf_op jit(solution)/shard_map/all_gather | solution.py:157
  53.8 379.6 %all-gather.16.cloned.1.call-start = ((), (), s32[]{:S(2)}) async-start(), calls=%async_computation.9 | async-start | bytes 5898240 | tf_op jit(solution)/shard_map/all_gather | solution.py:161
  54.4 400.1 %all-gather.18.cloned.1.call-start = ((), (), s32[]{:S(2)}) async-start(), calls=%async_computation.10 | async-start | bytes 5898240 | tf_op jit(solution)/shard_map/all_gather | solution.py:163
  55.0 1008.1 %reduce-scatter.8.cloned.1.call-start = ((), (), s32[]{:S(2)}) async-start(), calls=%async_computation.11 | async-start | bytes 14155776 | tf_op jit(solution)/shard_map/reduce_scatter | solution.py:258
  55.2 422.3 %copy-start.35 = (f32[768]{0:T(1024)}, f32[768]{0:T(1024)S(1)}, u32[]{:S(2)}) copy-start(f32[768]{0:T(1024)S(1)} %convert_element_type.228) | copy-start | bytes 9220
  55.3 399.3 %copy-start.45 = (f32[768]{0:T(1024)}, f32[768]{0:T(1024)S(1)}, u32[]{:S(2)}) copy-start(f32[768]{0:T(1024)S(1)} %convert_element_type.229) | copy-start | bytes 9220
  60.7 402.1 %copy-start.26 = (f32[768]{0:T(1024)}, f32[768]{0:T(1024)S(1)}, u32[]{:S(2)}) copy-start(f32[768]{0:T(1024)S(1)} %convert_element_type.234) | copy-start | bytes 9220
  267.8 9.0 copy-start
  289.6 8.3 copy-start
  310.8 9.8 copy-start
  333.4 8.3 copy-start
  429.2 25.2 %copy-start.18 = (bf16[512,12,64]{0,2,1:T(8,128)(2,1)}, bf16[512,12,64]{0,2,1:T(8,128)(2,1)S(1)}, u32[]{:S(2)}) copy-start(bf16[512,12,64]{0,2,1:T(8,128)(2,1)S(1)} %fusion.44) | copy-start | bytes 2359300
  432.0 45.6 %copy-start.33 = (f32[512]{0:T(512)}, f32[512]{0:T(512)S(1)}, u32[]{:S(2)}) copy-start(f32[512]{0:T(512)S(1)} %broadcast_multiply_fusion.1) | copy-start | bytes 6148
  433.4 44.1 %copy-start.42 = (f32[512]{0:T(512)}, f32[512]{0:T(512)S(1)}, u32[]{:S(2)}) copy-start(f32[512]{0:T(512)S(1)} %fusion.45) | copy-start | bytes 6148
  463.4 10.4 slice-start
  464.3 9.6 copy-start.21
  465.1 8.8 copy-start.13
  465.1 8.8 slice-start.1
  513.3 18.1 %copy-start.5 = (bf16[1,512,768]{1,2,0:T(8,128)(2,1)S(1)}, bf16[1,512,768]{1,2,0:T(8,128)(2,1)}, u32[]{:S(2)}) copy-start(bf16[1,512,768]{1,2,0:T(8,128)(2,1)} %copy-done.4) | copy-start | bytes 2359300 | tf_op jit(solution)/shard_map/while
  558.9 18.1 %copy-start.5 = (bf16[1,512,768]{1,2,0:T(8,128)(2,1)S(1)}, bf16[1,512,768]{1,2,0:T(8,128)(2,1)}, u32[]{:S(2)}) copy-start(bf16[1,512,768]{1,2,0:T(8,128)(2,1)} %copy-done.4) | copy-start | bytes 2359300 | tf_op jit(solution)/shard_map/while
  604.9 18.2 %copy-start.5 = (bf16[1,512,768]{1,2,0:T(8,128)(2,1)S(1)}, bf16[1,512,768]{1,2,0:T(8,128)(2,1)}, u32[]{:S(2)}) copy-start(bf16[1,512,768]{1,2,0:T(8,128)(2,1)} %copy-done.4) | copy-start | bytes 2359300 | tf_op jit(solution)/shard_map/while
  650.9 18.2 %copy-start.5 = (bf16[1,512,768]{1,2,0:T(8,128)(2,1)S(1)}, bf16[1,512,768]{1,2,0:T(8,128)(2,1)}, u32[]{:S(2)}) copy-start(bf16[1,512,768]{1,2,0:T(8,128)(2,1)} %copy-done.4) | copy-start | bytes 2359300 | tf_op jit(solution)/shard_map/while
  696.9 18.2 %copy-start.5 = (bf16[1,512,768]{1,2,0:T(8,128)(2,1)S(1)}, bf16[1,512,768]{1,2,0:T(8,128)(2,1)}, u32[]{:S(2)}) copy-start(bf16[1,512,768]{1,2,0:T(8,128)(2,1)} %copy-done.4) | copy-start | bytes 2359300 | tf_op jit(solution)/shard_map/while
  743.0 18.1 %copy-start.5 = (bf16[1,512,768]{1,2,0:T(8,128)(2,1)S(1)}, bf16[1,512,768]{1,2,0:T(8,128)(2,1)}, u32[]{:S(2)}) copy-start(bf16[1,512,768]{1,2,0:T(8,128)(2,1)} %copy-done.4) | copy-start | bytes 2359300 | tf_op jit(solution)/shard_map/while
  788.9 18.1 %copy-start.5 = (bf16[1,512,768]{1,2,0:T(8,128)(2,1)S(1)}, bf16[1,512,768]{1,2,0:T(8,128)(2,1)}, u32[]{:S(2)}) copy-start(bf16[1,512,768]{1,2,0:T(8,128)(2,1)} %copy-done.4) | copy-start | bytes 2359300 | tf_op jit(solution)/shard_map/while
  834.9 16.9 %copy-start.5 = (bf16[1,512,768]{1,2,0:T(8,128)(2,1)S(1)}, bf16[1,512,768]{1,2,0:T(8,128)(2,1)}, u32[]{:S(2)}) copy-start(bf16[1,512,768]{1,2,0:T(8,128)(2,1)} %copy-done.4) | copy-start | bytes 2359300 | tf_op jit(solution)/shard_map/while
  857.4 253.3 %reduce-scatter.16.cloned.1.call-start = ((), (), s32[]{:S(2)}) async-start(), calls=%async_computation.15 | async-start | bytes 4423680
  1071.1 67.9 %reduce-scatter.10.cloned.1.call-start = ((), (), s32[]{:S(2)}) async-start(), calls=%async_computation.12 | async-start | bytes 1474560 | tf_op jit(solution)/shard_map/reduce_scatter | solution.py:286
  1074.2 115.1 %reduce-scatter.14.cloned.1.call-start = ((), (), s32[]{:S(2)}) async-start(), calls=%async_computation.14 | async-start | bytes 5898240 | tf_op jit(solution)/shard_map/reduce_scatter | solution.py:304
  1081.8 158.1 %reduce-scatter.12.cloned.1.call-start = ((), (), s32[]{:S(2)}) async-start(), calls=%async_computation.13 | async-start | bytes 5898240 | tf_op jit(solution)/shard_map/reduce_scatter | solution.py:298
  1089.7 150.2 %copy-start.10 = (bf16[1,512,768]{2,1,0:T(8,128)(2,1)S(1)}, bf16[1,512,768]{2,1,0:T(8,128)(2,1)}, u32[]{:S(2)}) copy-start(bf16[1,512,768]{2,1,0:T(8,128)(2,1)} %param.35) | copy-start | bytes 2359300
  1089.7 151.7 %copy-start.52 = (bf16[192]{0:T(256)(128)(2,1)S(1)}, bf16[192]{0:T(256)(128)(2,1)}, u32[]{:S(2)}) copy-start(bf16[192]{0:T(256)(128)(2,1)} %param.34) | copy-start | bytes 1156
  1089.7 153.3 %copy-start.37 = (bf16[768]{0:T(1024)(128)(2,1)S(1)}, bf16[768]{0:T(1024)(128)(2,1)}, u32[]{:S(2)}) copy-start(bf16[768]{0:T(1024)(128)(2,1)} %get-tuple-element.519) | copy-start | bytes 4612
  1089.7 153.3 %copy-start.38 = (bf16[768]{0:T(1024)(128)(2,1)S(1)}, bf16[768]{0:T(1024)(128)(2,1)}, u32[]{:S(2)}) copy-start(bf16[768]{0:T(1024)(128)(2,1)} %get-tuple-element.598) | copy-start | bytes 4612
  1089.7 153.3 %copy-start.39 = (bf16[768]{0:T(1024)(128)(2,1)S(1)}, bf16[768]{0:T(1024)(128)(2,1)}, u32[]{:S(2)}) copy-start(bf16[768]{0:T(1024)(128)(2,1)} %get-tuple-element.602) | copy-start | bytes 4612
  1089.8 153.3 %copy-start.44 = (bf16[3072]{0:T(1024)(128)(2,1)S(1)}, bf16[3072]{0:T(1024)(128)(2,1)}, u32[]{:S(2)}) copy-start(bf16[3072]{0:T(1024)(128)(2,1)} %get-tuple-element.600) | copy-start | bytes 18436
  1089.8 153.3 %copy-start.47 = (bf16[768]{0:T(1024)(128)(2,1)S(1)}, bf16[768]{0:T(1024)(128)(2,1)}, u32[]{:S(2)}) copy-start(bf16[768]{0:T(1024)(128)(2,1)} %get-tuple-element.517) | copy-start | bytes 4612
  1089.8 153.3 %copy-start.48 = (bf16[768]{0:T(1024)(128)(2,1)S(1)}, bf16[768]{0:T(1024)(128)(2,1)}, u32[]{:S(2)}) copy-start(bf16[768]{0:T(1024)(128)(2,1)} %get-tuple-element.521) | copy-start | bytes 4612
  1089.8 192.6 %copy-start.8 = (f32[512,768]{1,0:T(8,128)S(1)}, f32[512,768]{1,0:T(8,128)}, u32[]{:S(2)}) copy-start(f32[512,768]{1,0:T(8,128)} %copy-done.7) | copy-start | bytes 4718596
  1089.8 192.6 %copy-start.27 = (f32[768]{0:T(1024)S(1)}, f32[768]{0:T(1024)}, u32[]{:S(2)}) copy-start(f32[768]{0:T(1024)} %copy-done.26) | copy-start | bytes 9220
  1089.8 192.6 %copy-start.30 = (f32[512]{0:T(512)S(1)}, f32[512]{0:T(512)}, u32[]{:S(2)}) copy-start(f32[512]{0:T(512)} %copy-done.29) | copy-start | bytes 6148
  1089.8 192.6 %copy-start.32 = (f32[512]{0:T(512)S(1)}, f32[512]{0:T(512)}, u32[]{:S(2)}) copy-start(f32[512]{0:T(512)} %copy-done.31) | copy-start | bytes 6148
  1089.8 302.2 %all-reduce.23.cloned.1.call-start = ((), (), s32[]{:S(2)}) async-start(), calls=%async_computation.16 | async-start | bytes 7667712 | tf_op jit(solution)/shard_map/psum | solution.py:318
  1239.8 43.8 %copy-start.20 = (bf16[512,12,64]{0,2,1:T(8,128)(2,1)S(1)}, bf16[512,12,64]{0,2,1:T(8,128)(2,1)}, u32[]{:S(2)}) copy-start(bf16[512,12,64]{0,2,1:T(8,128)(2,1)} %get-tuple-element.605) | copy-start | bytes 2359300
  1239.9 43.8 %copy-start.41 = (f32[512]{0:T(512)S(1)}, f32[512]{0:T(512)}, u32[]{:S(2)}) copy-start(f32[512]{0:T(512)} %copy-done.40) | copy-start | bytes 6148
  (62 other events, 222.1 us)
Sparse Core Ops, SparseCore 0:
  9.5 33.6 all-gather.7
  50.9 98.7 all-gather.11
  152.5 96.8 all-gather.9
  250.8 15.6 all-gather.13
  267.9 37.4 all-gather.15
  306.8 37.4 all-gather.17
  857.5 205.5 reduce-scatter.7
  1071.2 39.4 reduce-scatter.15
  1113.3 25.6 reduce-scatter.9
  1141.3 47.9 reduce-scatter.13
  1191.8 47.9 reduce-scatter.11
  1244.3 147.7 all-reduce.22
where the time goes:
time: 1420 us; the launch traced here: 1410 us
  waiting for transfers between devices  649 us (46%)
  matrix products  374 us (26%)
  local copies, waits for them, and re-layouts  220 us (15%)
  other arithmetic  75.2 us (5%)
  blocking collectives  52.7 us (4%)
  loops' own time  17.1 us (1%)
  between operations  17.1 us (1%)
    reduce_scatter x1, waiting for transfers between devices, body(): lax.psum_scatter(key_terms.astype(jnp.bfloat16), 'ctx', scatter_dimension...  203 us
    dynamic_update_slice x8, local copies, waits for them, and re-layouts, backward_core(): key_terms = lax.dynamic_update_slice(key_terms, joined, (offset, 0))  116 us
    psum x1, waiting for transfers between devices, body(): lax.psum(shards[0].astype(jnp.bfloat16), 'ctx').astype(jnp.float32)  102 us
    all_gather x1, waiting for transfers between devices, body(): lax.all_gather(key_low, 'ctx', axis=0, tiled=True)  91.1 us
    all_gather x1, waiting for transfers between devices, body(): lax.all_gather(value_low, 'ctx', axis=0, tiled=True)  88.8 us
    dot_general x8, matrix products, forward_core(): jnp.einsum('hqk,khd->qhd', weights.astype(jnp.bfloat16), value_heads, pre...  53.2 us
    dot_general x8, matrix products, forward_core(): jnp.einsum('qhd,khd->hqk', query_heads, key_heads, preferred_element_type...  52.6 us
    reduce_scatter x1, waiting for transfers between devices, body(): lax.psum_scatter(grad_in_full.astype(jnp.bfloat16), 'fsdp', scatter_dimen...  50.5 us
  transfers between devices with their start and end apart: 12, of which 9 were waited for; matrix products, arithmetic and copies ran while one was open for 17% of the time, Pallas kernels for 0%

commit v1 on v0

--- a/solution.py
+++ b/solution.py
@@ -4,6 +4,7 @@
 import jax.numpy as jnp
 from jax import lax
 from jax.sharding import PartitionSpec as P
+from jax.lax import all_gather
 
 H = 12
 HD = 64
@@ -136,6 +137,11 @@
     norm2_bias,
     cotangent,
 ):
+
+    def _cut_classes(view):
+        answer = all_gather(view, "ctx")
+        return jnp.sum(answer, axis=0)
+
     (
         qkv_full,
         query_shift,
@@ -315,7 +321,7 @@
         ).astype(jnp.float32),
     )
     totals = (
-        lax.psum(shards[0].astype(jnp.bfloat16), "ctx").astype(jnp.float32),
+        _cut_classes(shards[0].astype(jnp.bfloat16)).astype(jnp.float32),
         lax.psum(shards[1].astype(jnp.bfloat16), "ctx").astype(jnp.float32),
         lax.psum(shards[2].astype(jnp.bfloat16), "ctx").astype(jnp.float32),
         lax.psum(shards[3].astype(jnp.bfloat16), "ctx").astype(jnp.float32),

time: 1420 us -> 1490 us (1.049)
  waiting for transfers between devices: 649 us -> 721 us
    all_gather x0 -> x1, waiting for transfers between devices: none -> 57.7 us  [_cut_classes(): answer = all_gather(view, 'ctx')]
    reduce_scatter x0 -> x1, waiting for transfers between devices: none -> 42.9 us  [body(): lax.psum_scatter(grad_qkv_full.astype(jnp.bfloat16), 'fsdp', scatter_dime...]
    unnamed x13, waiting for transfers between devices: 23.2 us -> 2.41 us
    reduce_scatter x1, waiting for transfers between devices: 203 us -> 185 us  [body(): lax.psum_scatter(key_terms.astype(jnp.bfloat16), 'ctx', scatter_dimension...]
    psum x1, waiting for transfers between devices: 102 us -> 118 us  [body(): lax.psum(shards[3].astype(jnp.bfloat16), 'ctx').astype(jnp.float32)]
    unnamed x132 -> x130, local copies, waits for them, and re-layouts: 43.5 us -> 39.6 us
  transfers between devices with their start and end apart: 12 -> 13, of which waited for: 9 -> 10; matrix products, arithmetic and copies ran while one was open for 17% -> 17% of each run, Pallas kernels for 0% -> 0%
where the time goes in v1:
time: 1490 us; the launch traced here: 1480 us
  waiting for transfers between devices  721 us (48%)
  matrix products  374 us (25%)
  local copies, waits for them, and re-layouts  216 us (14%)
  other arithmetic  79.8 us (5%)
  blocking collectives  52.2 us (4%)
  loops' own time  17.1 us (1%)
  between operations  16.8 us (1%)
    reduce_scatter x1, waiting for transfers between devices, body(): lax.psum_scatter(key_terms.astype(jnp.bfloat16), 'ctx', scatter_dimension...  185 us
    psum x1, waiting for transfers between devices, body(): lax.psum(shards[3].astype(jnp.bfloat16), 'ctx').astype(jnp.float32)  118 us
    dynamic_update_slice x8, local copies, waits for them, and re-layouts, backward_core(): key_terms = lax.dynamic_update_slice(key_terms, joined, (offset, 0))  116 us
    all_gather x1, waiting for transfers between devices, body(): lax.all_gather(key_low, 'ctx', axis=0, tiled=True)  91.1 us
    all_gather x1, waiting for transfers between devices, body(): lax.all_gather(value_low, 'ctx', axis=0, tiled=True)  88.8 us
    all_gather x1, waiting for transfers between devices, _cut_classes(): answer = all_gather(view, 'ctx')  57.7 us
    dot_general x8, matrix products, forward_core(): jnp.einsum('hqk,khd->qhd', weights.astype(jnp.bfloat16), value_heads, pre...  53.2 us
    dot_general x8, matrix products, forward_core(): jnp.einsum('qhd,khd->hqk', query_heads, key_heads, preferred_element_type...  52.6 us
  transfers between devices with their start and end apart: 13, of which 10 were waited for; matrix products, arithmetic and copies ran while one was open for 17% of the time, Pallas kernels for 0%

profile of v1, /device:TPU:0, one launch (start us, length us, event | category | flops | bytes accessed | tf_op | source)
XLA Modules:
  0.0 1477.7 jit_solution(13727942647578431675)
XLA Ops:
  15.8 13.9 all-reduce.20
  29.7 13.5 all-gather.10.cloned.1.call-done
  61.0 88.8 %all-gather.14.cloned.1.call-done = bf16[4096,768]{1,0:T(8,128)(2,1)} async-done(((bf16[512,768]{1,0:T(8,128)(2,1)}), bf16[4096,768]{1,0:T(8,128)(2,1)}) %all-gather.14.cloned.1.call-update) | async-done | bytes 6291472 | tf_op jit(solution)/shard_map/all_gather | solution.py:198
  149.7 8.6 copy.75
  158.3 91.1 %all-gather.12.cloned.1.call-done = bf16[4096,768]{1,0:T(8,128)(2,1)} async-done(((bf16[512,768]{1,0:T(8,128)(2,1)}), bf16[4096,768]{1,0:T(8,128)(2,1)}) %all-gather.12.cloned.1.call-update) | async-done | bytes 6291472 | tf_op jit(solution)/shard_map/all_gather | solution.py:197
  249.4 8.7 copy.74
  258.1 170.9 %while.32 = (s32[]{:T(128)}, f32[12,512]{1,0:T(8,128)S(1)}, f32[12,512]{1,0:T(8,128)S(1)}, f32[512,12,64]{0,2,1:T(8,128)S(1)}, s32[512]{0:T(512)S(1)}, /*index=5...) while((s32[]{:T(128)}, f32[12,512]{1,0:T(8,128)S(1)}, ...), condition=%wide.region_5.6_spmd.clone, body=%wide.region_1.5_spmd.clone.sunk | while | flops 847692288 | bytes 98187464 | solution.py:39
  261.2 6.6 fusion.120
  267.8 6.5 bitcast_add_fusion.4
  283.0 6.6 fusion.120
  289.6 6.5 bitcast_add_fusion.4
  304.2 6.6 fusion.120
  310.8 7.6 bitcast_add_fusion.4
  326.8 6.6 fusion.120
  333.4 6.6 bitcast_add_fusion.4
  348.0 6.6 fusion.120
  354.6 6.5 bitcast_add_fusion.4
  369.0 6.6 fusion.120
  375.6 6.5 bitcast_add_fusion.4
  390.0 6.6 fusion.120
  396.6 6.5 bitcast_add_fusion.4
  411.0 6.6 fusion.120
  417.6 6.5 bitcast_add_fusion.4
  433.5 21.0 %multiply_convert_fusion = (bf16[512,3072]{1,0:T(8,128)(2,1)}, f32[512,3072]{1,0:T(8,128)}, f32[512,3072]{1,0:T(8,128)}) fusion(f32[3072]{0:T(1024)S(1)} %bitcast.197, bf16[768,3072]{1,0:T(8,128)(2,1)} %all-gather.18.cloned.1.call-done, f32[512,768]{1,0:T(8,128)} %copy-done.13, f32[768]{0:T(1024)S(1)} %convert_element_type.231, ...), kind=kOutput, calls=%fused_computation.47 | convolution fusion | flops 2521694208 | bytes 22042624 | tf_op jit(solution)/shard_map/dot_general | solution.py:214
  454.5 6.5 fusion.61
  465.1 8.7 fusion.53
  484.5 6.1 broadcast_in_dim.113
  490.7 366.6 %while.33 = (s32[]{:T(128)}, f32[512,12,64]{0,2,1:T(8,128)}, bf16[4096,1536]{0,1:T(8,128)(2,1)}, bf16[8,512,768]{1,2,0:T(8,128)(2,1)}, s32[512]{0:T(512)S(1)}, /...) while((s32[]{:T(128)}, f32[512,12,64]{0,2,1:T(8,128)}, ...), condition=%wide.region_17.18_spmd.clone, body=%wide.region_15.17_spmd.clone.sunk | while | flops 2058367488 | bytes 114907512 | solution.py:39
  516.8 14.6 dynamic_update_slice.8
  562.3 14.7 dynamic_update_slice.8
  608.3 14.7 dynamic_update_slice.8
  654.3 14.7 dynamic_update_slice.8
  700.4 14.7 dynamic_update_slice.8
  746.3 14.6 dynamic_update_slice.8
  792.3 14.6 dynamic_update_slice.8
  838.2 13.5 dynamic_update_slice.8
  860.5 6.8 convolution_convert_fusion
  868.7 6.7 convolution_convert_fusion.1
  877.8 185.1 %reduce-scatter.8.cloned.1.call-done = bf16[512,1536]{0,1:T(8,128)(2,1)} async-done(((bf16[4096,1536]{0,1:T(8,128)(2,1)}), bf16[512,1536]{0,1:T(8,128)(2,1)}) %reduce-scatter.8.cloned.1.call-update) | async-done | bytes 1572880 | tf_op jit(solution)/shard_map/reduce_scatter | solution.py:264
  1070.9 20.0 %reduce-scatter.10.cloned.1.call-done = bf16[192,768]{1,0:T(8,128)(2,1)} async-done(((bf16[768,768]{1,0:T(8,128)(2,1)}), bf16[192,768]{1,0:T(8,128)(2,1)}) %reduce-scatter.10.cloned.1.call-update) | async-done | bytes 294928 | tf_op jit(solution)/shard_map/reduce_scatter | solution.py:292
  1090.8 50.6 %reduce-scatter.14.cloned.1.call-done = bf16[768,768]{1,0:T(8,128)(2,1)} async-done(((bf16[3072,768]{1,0:T(8,128)(2,1)}), bf16[768,768]{1,0:T(8,128)(2,1)}) %reduce-scatter.14.cloned.1.call-update) | async-done | bytes 1179664 | tf_op jit(solution)/shard_map/reduce_scatter | solution.py:310
  1141.4 50.4 %reduce-scatter.12.cloned.1.call-done = bf16[192,3072]{1,0:T(8,128)(2,1)} async-done(((bf16[768,3072]{1,0:T(8,128)(2,1)}), bf16[192,3072]{1,0:T(8,128)(2,1)}) %reduce-scatter.12.cloned.1.call-update) | async-done | bytes 1179664 | tf_op jit(solution)/shard_map/reduce_scatter | solution.py:304
  1191.9 42.9 %reduce-scatter.16.cloned.1.call-done = bf16[192,2304]{1,0:T(8,128)(2,1)} async-done(((bf16[768,2304]{1,0:T(8,128)(2,1)}), bf16[192,2304]{1,0:T(8,128)(2,1)}) %reduce-scatter.16.cloned.1.call-update) | async-done | bytes 884752 | tf_op jit(solution)/shard_map/reduce_scatter | solution.py:283
  1236.6 118.5 %all-reduce.23.cloned.1.call-done = (bf16[192,768]{1,0:T(8,128)(2,1)}, bf16[192,3072]{1,0:T(8,128)(2,1)}, bf16[768,768]{1,0:T(8,128)(2,1)}) async-done(((bf16[192,768]{1,0:T(8,128)(2,1)}, bf16[192,3072]{1,0:T(8,128)(2,1)}, bf16[768,768]{1,0:T(8,128)(2,1)}), (bf16[192,768]{1,0:T(8,128)(2,1)}, bf16[192,3072]{1,0:T(8,128)(2,1)}, bf16[768,768]{1,0:T(8,128)(2,1)})) %all-reduce.23.cloned.1.call-update) | async-done | bytes 2654224 | tf_op jit(solution)/shard_map/psum | solution.py:327
  1360.9 10.7 all-reduce.19
  1372.3 22.3 %all-reduce.17 = (bf16[192]{0:T(256)(128)(2,1)S(1)}, bf16[192]{0:T(256)(128)(2,1)S(1)}, bf16[192]{0:T(256)(128)(2,1)S(1)}, bf16[192]{0:T(256)(128)(2,1)S(1)}, bf...) all-reduce(bf16[192]{0:T(256)(128)(2,1)S(1)} %dynamic-slice.9, ...), channel_id=1, replica_groups=mesh['ctx'=8,'fsdp'=4] {'ctx'}, use_global_device_ids=true, to_apply=%region_23.24 | all-reduce | flops 2304 | bytes 9216 | tf_op jit(solution)/shard_map/psum | solution.py:325
  1400.9 6.6 add_bitcast_fusion
  1407.5 57.7 %all-gather.22.cloned.1.call-done = bf16[1536,2304]{1,0:T(8,128)(2,1)} async-done(((bf16[192,2304]{1,0:T(8,128)(2,1)}), bf16[1536,2304]{1,0:T(8,128)(2,1)}) %all-gather.22.cloned.1.call-update) | async-done | bytes 7077904 | tf_op jit(solution)/shard_map/all_gather | solution.py:142
  (495 shorter events, 376.8 us)
Async XLA Ops:
  7.2 36.0 %all-gather.10.cloned.1.call-start = ((), (), s32[]{:S(2)}) async-start(), calls=%async_computation.5 | async-start | bytes 4423680 | tf_op jit(solution)/shard_map/all_gather | solution.py:160
  7.9 141.8 %all-gather.14.cloned.1.call-start = ((), (), s32[]{:S(2)}) async-start(), calls=%async_computation.7 | async-start | bytes 7077888 | tf_op jit(solution)/shard_map/all_gather | solution.py:198
  50.8 198.6 %all-gather.12.cloned.1.call-start = ((), (), s32[]{:S(2)}) async-start(), calls=%async_computation.6 | async-start | bytes 7077888 | tf_op jit(solution)/shard_map/all_gather | solution.py:197
  53.3 376.0 %all-gather.16.cloned.1.call-start = ((), (), s32[]{:S(2)}) async-start(), calls=%async_computation.8 | async-start | bytes 1474560 | tf_op jit(solution)/shard_map/all_gather | solution.py:163
  53.8 379.6 %all-gather.18.cloned.1.call-start = ((), (), s32[]{:S(2)}) async-start(), calls=%async_computation.9 | async-start | bytes 5898240 | tf_op jit(solution)/shard_map/all_gather | solution.py:167
  54.4 400.1 %all-gather.20.cloned.1.call-start = ((), (), s32[]{:S(2)}) async-start(), calls=%async_computation.10 | async-start | bytes 5898240 | tf_op jit(solution)/shard_map/all_gather | solution.py:169
  55.0 1008.0 %reduce-scatter.8.cloned.1.call-start = ((), (), s32[]{:S(2)}) async-start(), calls=%async_computation.11 | async-start | bytes 14155776 | tf_op jit(solution)/shard_map/reduce_scatter | solution.py:264
  55.2 422.3 %copy-start.35 = (f32[768]{0:T(1024)}, f32[768]{0:T(1024)S(1)}, u32[]{:S(2)}) copy-start(f32[768]{0:T(1024)S(1)} %convert_element_type.230) | copy-start | bytes 9220
  55.3 399.3 %copy-start.45 = (f32[768]{0:T(1024)}, f32[768]{0:T(1024)S(1)}, u32[]{:S(2)}) copy-start(f32[768]{0:T(1024)S(1)} %convert_element_type.231) | copy-start | bytes 9220
  60.7 402.1 %copy-start.26 = (f32[768]{0:T(1024)}, f32[768]{0:T(1024)S(1)}, u32[]{:S(2)}) copy-start(f32[768]{0:T(1024)S(1)} %convert_element_type.236) | copy-start | bytes 9220
  267.8 9.0 copy-start
  289.6 8.3 copy-start
  310.8 9.8 copy-start
  333.4 8.3 copy-start
  354.6 8.2 copy-start
  375.6 8.2 copy-start
  396.6 8.2 copy-start
  417.6 8.2 copy-start
  429.2 25.2 %copy-start.18 = (bf16[512,12,64]{0,2,1:T(8,128)(2,1)}, bf16[512,12,64]{0,2,1:T(8,128)(2,1)S(1)}, u32[]{:S(2)}) copy-start(bf16[512,12,64]{0,2,1:T(8,128)(2,1)S(1)} %fusion.44) | copy-start | bytes 2359300
  432.0 45.6 %copy-start.33 = (f32[512]{0:T(512)}, f32[512]{0:T(512)S(1)}, u32[]{:S(2)}) copy-start(f32[512]{0:T(512)S(1)} %broadcast_multiply_fusion.1) | copy-start | bytes 6148
  433.4 44.1 %copy-start.42 = (f32[512]{0:T(512)}, f32[512]{0:T(512)S(1)}, u32[]{:S(2)}) copy-start(f32[512]{0:T(512)S(1)} %fusion.45) | copy-start | bytes 6148
  454.5 6.9 copy-start.9
  463.4 10.4 slice-start
  464.2 9.6 copy-start.20
  465.1 8.8 copy-start.14
  465.1 8.8 slice-start.1
  513.3 18.1 %copy-start.5 = (bf16[1,512,768]{1,2,0:T(8,128)(2,1)S(1)}, bf16[1,512,768]{1,2,0:T(8,128)(2,1)}, u32[]{:S(2)}) copy-start(bf16[1,512,768]{1,2,0:T(8,128)(2,1)} %copy-done.4) | copy-start | bytes 2359300 | tf_op jit(solution)/shard_map/while
  558.8 18.1 %copy-start.5 = (bf16[1,512,768]{1,2,0:T(8,128)(2,1)S(1)}, bf16[1,512,768]{1,2,0:T(8,128)(2,1)}, u32[]{:S(2)}) copy-start(bf16[1,512,768]{1,2,0:T(8,128)(2,1)} %copy-done.4) | copy-start | bytes 2359300 | tf_op jit(solution)/shard_map/while
  604.8 18.2 %copy-start.5 = (bf16[1,512,768]{1,2,0:T(8,128)(2,1)S(1)}, bf16[1,512,768]{1,2,0:T(8,128)(2,1)}, u32[]{:S(2)}) copy-start(bf16[1,512,768]{1,2,0:T(8,128)(2,1)} %copy-done.4) | copy-start | bytes 2359300 | tf_op jit(solution)/shard_map/while
  650.8 18.2 %copy-start.5 = (bf16[1,512,768]{1,2,0:T(8,128)(2,1)S(1)}, bf16[1,512,768]{1,2,0:T(8,128)(2,1)}, u32[]{:S(2)}) copy-start(bf16[1,512,768]{1,2,0:T(8,128)(2,1)} %copy-done.4) | copy-start | bytes 2359300 | tf_op jit(solution)/shard_map/while
  696.9 18.2 %copy-start.5 = (bf16[1,512,768]{1,2,0:T(8,128)(2,1)S(1)}, bf16[1,512,768]{1,2,0:T(8,128)(2,1)}, u32[]{:S(2)}) copy-start(bf16[1,512,768]{1,2,0:T(8,128)(2,1)} %copy-done.4) | copy-start | bytes 2359300 | tf_op jit(solution)/shard_map/while
  742.9 18.1 %copy-start.5 = (bf16[1,512,768]{1,2,0:T(8,128)(2,1)S(1)}, bf16[1,512,768]{1,2,0:T(8,128)(2,1)}, u32[]{:S(2)}) copy-start(bf16[1,512,768]{1,2,0:T(8,128)(2,1)} %copy-done.4) | copy-start | bytes 2359300 | tf_op jit(solution)/shard_map/while
  788.8 18.1 %copy-start.5 = (bf16[1,512,768]{1,2,0:T(8,128)(2,1)S(1)}, bf16[1,512,768]{1,2,0:T(8,128)(2,1)}, u32[]{:S(2)}) copy-start(bf16[1,512,768]{1,2,0:T(8,128)(2,1)} %copy-done.4) | copy-start | bytes 2359300 | tf_op jit(solution)/shard_map/while
  834.7 16.9 %copy-start.5 = (bf16[1,512,768]{1,2,0:T(8,128)(2,1)S(1)}, bf16[1,512,768]{1,2,0:T(8,128)(2,1)}, u32[]{:S(2)}) copy-start(bf16[1,512,768]{1,2,0:T(8,128)(2,1)} %copy-done.4) | copy-start | bytes 2359300 | tf_op jit(solution)/shard_map/while
  857.3 233.6 %reduce-scatter.10.cloned.1.call-start = ((), (), s32[]{:S(2)}) async-start(), calls=%async_computation.12 | async-start | bytes 1474560 | tf_op jit(solution)/shard_map/reduce_scatter | solution.py:292
  860.4 281.0 %reduce-scatter.14.cloned.1.call-start = ((), (), s32[]{:S(2)}) async-start(), calls=%async_computation.14 | async-start | bytes 5898240 | tf_op jit(solution)/shard_map/reduce_scatter | solution.py:310
  867.4 324.4 %reduce-scatter.12.cloned.1.call-start = ((), (), s32[]{:S(2)}) async-start(), calls=%async_computation.13 | async-start | bytes 5898240 | tf_op jit(solution)/shard_map/reduce_scatter | solution.py:304
  875.4 359.3 %reduce-scatter.16.cloned.1.call-start = ((), (), s32[]{:S(2)}) async-start(), calls=%async_computation.16 | async-start | bytes 4423680 | tf_op jit(solution)/shard_map/reduce_scatter | solution.py:283
  1070.8 164.0 %copy-start.10 = (bf16[1,512,768]{2,1,0:T(8,128)(2,1)S(1)}, bf16[1,512,768]{2,1,0:T(8,128)(2,1)}, u32[]{:S(2)}) copy-start(bf16[1,512,768]{2,1,0:T(8,128)(2,1)} %param.35) | copy-start | bytes 2359300
  1070.8 165.5 %copy-start.52 = (bf16[192]{0:T(256)(128)(2,1)S(1)}, bf16[192]{0:T(256)(128)(2,1)}, u32[]{:S(2)}) copy-start(bf16[192]{0:T(256)(128)(2,1)} %param.34) | copy-start | bytes 1156
  1070.8 284.3 %all-reduce.23.cloned.1.call-start = ((), (), s32[]{:S(2)}) async-start(), calls=%async_computation.17 | async-start | bytes 5308416 | tf_op jit(solution)/shard_map/psum | solution.py:327
  1191.8 273.4 %all-gather.22.cloned.1.call-start = ((), (), s32[]{:S(2)}) async-start(), calls=%async_computation.15 | async-start | bytes 7962624 | tf_op jit(solution)/shard_map/all_gather | solution.py:142
  1358.2 41.5 %copy-start.8 = (f32[512,768]{1,0:T(8,128)S(1)}, f32[512,768]{1,0:T(8,128)}, u32[]{:S(2)}) copy-start(f32[512,768]{1,0:T(8,128)} %copy-done.7) | copy-start | bytes 4718596
  1358.2 41.5 %copy-start.27 = (f32[768]{0:T(1024)S(1)}, f32[768]{0:T(1024)}, u32[]{:S(2)}) copy-start(f32[768]{0:T(1024)} %copy-done.26) | copy-start | bytes 9220
  1358.2 41.5 %copy-start.30 = (f32[512]{0:T(512)S(1)}, f32[512]{0:T(512)}, u32[]{:S(2)}) copy-start(f32[512]{0:T(512)} %copy-done.29) | copy-start | bytes 6148
  1358.2 41.5 %copy-start.32 = (f32[512]{0:T(512)S(1)}, f32[512]{0:T(512)}, u32[]{:S(2)}) copy-start(f32[512]{0:T(512)} %copy-done.31) | copy-start | bytes 6148
  1358.2 42.7 %copy-start.12 = (f32[512,768]{1,0:T(8,128)S(1)}, f32[512,768]{1,0:T(8,128)}, u32[]{:S(2)}) copy-start(f32[512,768]{1,0:T(8,128)} %copy-done.11) | copy-start | bytes 4718596
  1358.2 42.7 %copy-start.41 = (f32[512]{0:T(512)S(1)}, f32[512]{0:T(512)}, u32[]{:S(2)}) copy-start(f32[512]{0:T(512)} %copy-done.40) | copy-start | bytes 6148
  (63 other events, 219.9 us)
Sparse Core Ops, SparseCore 0:
  9.5 33.6 all-gather.9
  50.9 98.7 all-gather.13
  152.5 96.8 all-gather.11
  250.8 15.6 all-gather.15
  267.9 37.4 all-gather.17
  306.8 37.4 all-gather.19
  857.4 205.5 reduce-scatter.7
  1066.1 24.6 reduce-scatter.9
  1093.4 47.9 reduce-scatter.13
  1143.8 47.9 reduce-scatter.11
  1194.4 40.3 reduce-scatter.15
  1238.6 116.4 all-reduce.22
  1357.3 107.9 all-gather.21
